TPU v7x, 32 devices: a whole 2x2x4 slice. The times are simulated.
32 devices in a mesh: rep: 4 (over y, core), fsdp: 8 (over z, x).
Axes of the slice: x: 2, y: 2, z: 4, core: 2. Of those that a mesh axis runs over, the one named last changes fastest.
Arguments:
- activations: bfloat16 [4, 3072, 4096], P('rep', 'fsdp'), may hold values from -6 to 6
- key_cotangent: bfloat16 [4, 3072, 512], P('rep', 'fsdp'), may hold values from -12 to 12
- doc_ids: int32 [4, 3072], P('rep', 'fsdp'), may hold values from 0 to 7, as said below
- replica_params: float32 [4, 4096, 512], P('rep', 'fsdp'), may hold values from -14 to 14
- first_moment: float32 [4, 4096, 512], P('rep', 'fsdp'), may hold values from -6 to 6
- second_moment: float32 [4, 4096, 512], P('rep', 'fsdp'), may hold values from 1 to 16
- anchor: float32 [4096, 512], P(('fsdp', 'rep')), may hold values from -8 to 8
- momentum: float32 [4096, 512], P(('fsdp', 'rep')), may hold values from -3 to 3
Outputs:
- new_first: float32 [4, 4096, 512], P('rep', 'fsdp')
- new_second: float32 [4, 4096, 512], P('rep', 'fsdp')
- new_momentum: float32 [4096, 512], P(('fsdp', 'rep'))
- new_params: float32 [4096, 512], P('fsdp')
Inputs may be any that keep to these rules, and one draw needn't show every extreme that they name: `doc_ids`: within each group the numbers never fall along the tokens; every block of 384 consecutive tokens (from token 0) holds the first token of exactly one document; every document holds 1 to 767 tokens and one holds exactly 767.
All inputs are finite; a program needn't handle non-finite values.
Results may differ from a plain program's by a relative error of at most 0.0035.
Values may be sent and summed in bfloat16 or wider, within the bound.
No kernel may reach another device: no remote copies, remote signals or barrier semaphores. Data moves between devices by JAX's collectives and lax.ppermute only.
A program may use at most 64 MiB of HBM per device.

v0:
```python
import math
import jax
import jax.numpy as jnp
from jax import lax
from jax.sharding import PartitionSpec as P

KV_HEADS = 4
HEAD = 128
rope_base = 500000.0


def entering(array, axis, combine, identity):
    peers, index = (lax.axis_size(axis), lax.axis_index(axis))
    everything = jax.tree.map(lambda part: lax.all_gather(part, axis), array)
    start = jax.tree.map(
        lambda part, zero: jnp.broadcast_to(jnp.asarray(zero, part.dtype), part.shape),
        array,
        identity,
    )

    def hop(k, before):
        reached = k < index
        new = combine(before, jax.tree.map(lambda part: part[k], everything))
        return jax.tree.map(lambda a, b: jnp.where(reached, a, b), new, before)

    return lax.fori_loop(0, peers, hop, start)


def rotate_back(cotangent, offsets):
    row_count = cotangent.shape[0]
    half_head = HEAD // 2
    blocks = cotangent.astype(jnp.float32).reshape(row_count, KV_HEADS, 2, half_head)
    frequency = jnp.exp(
        jnp.arange(half_head, dtype=jnp.float32) * (-math.log(rope_base) / half_head)
    )
    angles = offsets[:, None] * frequency[None, :]
    cosine = jnp.cos(angles)[:, None, :]
    sine_part = jnp.sin(angles)[:, None, :]
    lower_half = blocks[:, :, 0, :]
    upper_half = blocks[:, :, 1, :]
    fresh_lower = lower_half * cosine + upper_half * sine_part
    fresh_upper = upper_half * cosine - lower_half * sine_part
    return (
        jnp.stack([fresh_lower, fresh_upper], axis=2)
        .reshape(row_count, KV_HEADS * HEAD)
        .astype(jnp.bfloat16)
    )


def inner_step(grad, params, first, second):
    fresh_first = 0.9 * first + 0.1 * grad
    fresh_second = 0.95 * second + 0.05 * grad * grad
    stepped = params - 0.2 * (fresh_first / (jnp.sqrt(fresh_second) + 1e-08) + 0.1 * params)
    return (fresh_first, fresh_second, stepped)


def join_runs(before, behind):
    joined_doc = jnp.where(behind[0] < 0, before[0], behind[0])
    joined_start = jnp.where(
        behind[0] < 0, before[1], jnp.where(behind[0] == before[0], before[1], behind[1])
    )
    return (joined_doc, joined_start)


def local(
    activations,
    key_cotangent,
    doc_ids,
    replica_params,
    first_moment,
    second_moment,
    anchor,
    momentum,
):
    features = activations[0]
    cotangent = key_cotangent[0]
    doc_block = doc_ids[0]
    tok_rows = features.shape[0]
    groups = lax.axis_size("fsdp")
    replicas = lax.axis_size("rep")
    device = lax.axis_index("fsdp")
    root = device * tok_rows
    places = jnp.arange(tok_rows, dtype=jnp.int32)
    last_doc = doc_block[tok_rows - 1]
    last_start = jnp.min(jnp.where(doc_block == last_doc, places, jnp.int32(tok_rows))) + root
    prior_doc, prior_start = entering(
        (last_doc, last_start), "fsdp", join_runs, (jnp.int32(-1), jnp.int32(0))
    )
    begins = jnp.concatenate([jnp.ones((1,), jnp.bool_), doc_block[1:] != doc_block[:-1]])
    local_start = lax.cummax(jnp.where(begins, places, jnp.int32(0)), axis=0) + root
    run_start = jnp.where(doc_block == prior_doc, prior_start, local_start)
    offsets = (root + places - run_start).astype(jnp.float32)
    rotated = rotate_back(cotangent, offsets)
    grad_scale = 1.0 / math.sqrt(tok_rows * groups)
    product = lax.dot_general(
        features, rotated, (((0,), (0,)), ((), ())), preferred_element_type=jnp.float32
    )
    grad = lax.psum_scatter(
        (product * grad_scale).astype(jnp.bfloat16), "fsdp", scatter_dimension=0, tiled=True
    ).astype(jnp.float32)
    fresh_first, fresh_second, stepped = inner_step(
        grad, replica_params[0], first_moment[0], second_moment[0]
    )
    share_rows = anchor.shape[0]
    summed = lax.psum(stepped, "rep")
    anchor_rows, momentum_rows = (
        lax.all_gather(anchor, "rep", axis=0, tiled=True),
        lax.all_gather(momentum, "rep", axis=0, tiled=True),
    )
    pseudo_grad = anchor_rows - summed / replicas
    momentum_full = 0.9 * momentum_rows + pseudo_grad
    new_params = anchor_rows - 0.7 * (pseudo_grad + 0.9 * momentum_full)
    new_momentum = lax.dynamic_slice_in_dim(
        momentum_full, lax.axis_index("rep") * share_rows, share_rows, 0
    )
    return (fresh_first[None], fresh_second[None], new_momentum, new_params)


def solution(mesh):
    placed = (
        P("rep", "fsdp", None),
        P("rep", "fsdp", None),
        P("rep", "fsdp"),
        P("rep", "fsdp", None),
        P("rep", "fsdp", None),
        P("rep", "fsdp", None),
        P(("fsdp", "rep"), None),
        P(("fsdp", "rep"), None),
    )
    return jax.shard_map(
        local,
        mesh=mesh,
        in_specs=placed,
        out_specs=(
            P("rep", "fsdp", None),
            P("rep", "fsdp", None),
            P(("fsdp", "rep"), None),
            P("fsdp", None),
        ),
        check_vma=False,
    )
```

profile of v0, /device:TPU:0, one launch (start us, length us, event | category | flops | bytes accessed | tf_op | source)
XLA Modules:
  0.0 208.1 jit_solution(2617310549342385104)
XLA Ops:
  8.0 0.0 copy-start
  8.0 0.0 reduce-scatter.2.cloned.1.call-start
  8.1 1.4 slice.28
  9.5 0.8 compare_reduce_fusion
  10.3 1.2 copy.22
  11.5 0.9 convert.9
  12.5 1.3 compare_reduce_fusion.2
  13.7 0.7 select_reduce_fusion
  14.4 1.2 dynamic-slice
  15.6 1.2 bitcast_dynamic-update-slice_fusion
  17.5 0.8 dynamic-update-slice.1
  18.3 13.1 %all-reduce.2 = (s32[8]{0:T(128)S(1)}, s32[8]{0:T(128)S(1)}) all-reduce(s32[8]{0:T(128)S(1)} %bitcast_dynamic-update-slice_fusion, s32[8]{0:T(128)S(1)} %dynamic-update-slice.1), channel_id=2, replica_groups=mesh['rep'=4,'fsdp'=8] {'fsdp'}, use_global_device_ids=true, to_apply=%add | all-reduce | flops 16 | bytes 128 | tf_op jit(solution)/shard_map/all_gather | solution.py:14
  31.3 27.6 %while.15 = (s32[]{:T(128)}, s32[]{:T(128)}, s32[]{:T(128)}, s32[]{:T(128)}, s32[8]{0:T(128)S(1)}, /*index=5*/s32[8]{0:T(128)S(1)}, s32[]{:T(128)}, s32[]{:T(128)}) while((s32[]{:T(128)}, s32[]{:T(128)}, s32[]{:T(128)}, s32[]{:T(128)}, s32[8]{0:T(128)S(1)}, /*index=5*/s32[8]{0:T(128)S(1)}, s32[]{:T(128)}, s32[]{:T(128)}) %tuple.39), condition=%wide.region_2.3_spmd, body=%wide.region_1.2_spmd.sunk | while | flops 10 | bytes 217 | solution.py:26
  31.3 0.6 dynamic_slice.21
  33.6 0.6 dynamic_slice.22
  34.8 0.6 dynamic_slice.21
  37.0 0.6 dynamic_slice.22
  38.2 0.6 dynamic_slice.21
  40.5 0.6 dynamic_slice.22
  41.7 0.6 dynamic_slice.21
  43.9 0.6 dynamic_slice.22
  45.1 0.6 dynamic_slice.21
  47.4 0.6 dynamic_slice.22
  48.6 0.6 dynamic_slice.21
  50.8 0.6 dynamic_slice.22
  52.0 0.6 dynamic_slice.21
  54.3 0.6 dynamic_slice.22
  55.5 0.6 dynamic_slice.21
  57.7 0.6 dynamic_slice.22
  58.9 0.7 compare_reduce_fusion.1
  59.6 0.1 add_select_fusion
  59.7 0.3 reduce-window.9
  60.0 0.1 slice.32
  60.1 0.1 slice_reduce_fusion
  60.2 0.1 fusion.9
  60.3 0.4 multiply_cosine_fusion
  60.7 1.2 add_convert_fusion
  62.0 0.0 copy-done
  62.0 4.3 %fusion = bf16[4096,512]{0,1:T(8,128)(2,1)} fusion(bf16[384,512]{0,1:T(8,128)(2,1)S(1)} %bitcast.56, bf16[1,384,4096]{2,1,0:T(8,128)(2,1)S(1)} %copy-done), kind=kOutput, calls=%fused_computation.1 | convolution fusion | flops 1614807040 | bytes 7733248 | tf_op jit(solution)/shard_map/dot_general | solution.py:95
  66.3 0.0 copy-start.1
  66.3 0.0 reduce-scatter.2.cloned.1.call-update
  66.3 0.0 all-gather.6.cloned.1.call-start
  66.4 0.9 copy-done.1
  67.3 0.8 copy.25
  68.1 0.0 all-gather.6.cloned.1.call-update
  68.1 0.0 all-gather.4.cloned.1.call-start
  68.2 1.8 copy.24
  70.0 0.0 all-gather.4.cloned.1.call-update
  70.0 0.0 all-reduce.5.cloned.1.call-start
  70.1 2.5 %copy.26 = f32[1,512,512]{1,2,0:T(8,128)} copy(f32[1,512,512]{2,1,0:T(8,128)} %param.13) | data formatting | bytes 2097152 | tf_op args[3]
  72.6 2.6 %copy.21 = f32[1,512,512]{1,2,0:T(8,128)} copy(f32[1,512,512]{2,1,0:T(8,128)} %param.14) | data formatting | bytes 2097152 | tf_op args[4]
  75.2 2.5 %copy.23 = f32[1,512,512]{1,2,0:T(8,128)} copy(f32[1,512,512]{2,1,0:T(8,128)} %param.15) | data formatting | bytes 2097152 | tf_op args[5]
  77.7 75.5 %reduce-scatter.2.cloned.1.call-done = bf16[512,512]{0,1:T(8,128)(2,1)} async-done(((bf16[4096,512]{0,1:T(8,128)(2,1)}), bf16[512,512]{0,1:T(8,128)(2,1)}) %reduce-scatter.2.cloned.1.call-update) | async-done | bytes 524304 | tf_op jit(solution)/shard_map/reduce_scatter | solution.py:98
  153.2 4.1 %bitcast_subtract_fusion = (f32[512,512]{0,1:T(8,128)}, f32[1,512,512]{1,2,0:T(8,128)}, f32[1,512,512]{1,2,0:T(8,128)}) fusion(f32[1,512,512]{1,2,0:T(8,128)} %copy.26, bf16[512,512]{0,1:T(8,128)(2,1)} %reduce-scatter.2.cloned.1.call-done, f32[1,512,512]{1,2,0:T(8,128)} %copy.21, f32[1,512,512]{1,2,0:T(8,128)} %copy.23), kind=kLoop, calls=%fused_computation.7 | loop fusion | flops 3670016 | bytes 6815744 | tf_op jit(solution)/shard_map/sub | solution.py:53
  157.3 0.0 all-reduce.5.cloned.1.call-update
  157.4 2.5 %copy.27 = f32[1,512,512]{2,1,0:T(8,128)} copy(f32[1,512,512]{1,2,0:T(8,128)} %get-tuple-element.142) | data formatting | bytes 2097152
  159.9 2.5 %copy.28 = f32[1,512,512]{2,1,0:T(8,128)} copy(f32[1,512,512]{1,2,0:T(8,128)} %get-tuple-element.141) | data formatting | bytes 2097152
  162.4 0.0 all-gather.6.cloned.1.call-done
  162.4 0.0 all-gather.4.cloned.1.call-done
  162.4 31.4 %all-reduce.5.cloned.1.call-done = f32[512,512]{0,1:T(8,128)} async-done(((f32[512,512]{0,1:T(8,128)}), f32[512,512]{0,1:T(8,128)}) %all-reduce.5.cloned.1.call-update) | async-done | bytes 1048592 | tf_op jit(solution)/shard_map/psum | solution.py:105
  193.8 3.3 %multiply_subtract_fusion = (f32[512,512]{0,1:T(8,128)}, f32[512,512]{0,1:T(8,128)S(1)}) fusion(f32[512,512]{0,1:T(8,128)} %all-gather.6.cloned.1.call-done, f32[512,512]{0,1:T(8,128)} %all-reduce.5.cloned.1.call-done, f32[512,512]{0,1:T(8,128)} %all-gather.4.cloned.1.call-done), kind=kLoop, calls=%fused_computation.11 | loop fusion | flops 2097152 | bytes 5242880 | tf_op jit(solution)/shard_map/sub | solution.py:112
  197.2 0.8 copy.29
  198.0 2.5 %copy.30 = f32[512,512]{1,0:T(8,128)} copy(f32[512,512]{0,1:T(8,128)} %get-tuple-element.138) | data formatting | bytes 2097152
  (6 shorter events, 0.1 us)
Async XLA Ops:
  8.0 54.0 %copy-start = (bf16[1,384,4096]{2,1,0:T(8,128)(2,1)S(1)}, bf16[1,384,4096]{2,1,0:T(8,128)(2,1)}, u32[]{:S(2)}) copy-start(bf16[1,384,4096]{2,1,0:T(8,128)(2,1)} %param.10) | copy-start | bytes 9437188
  8.0 145.2 %reduce-scatter.2.cloned.1.call-start = ((), (), s32[]{:S(2)}) async-start(), calls=%async_computation.1 | async-start | bytes 4718592 | tf_op jit(solution)/shard_map/reduce_scatter | solution.py:98
  66.3 0.9 copy-start.1
  66.3 96.1 %all-gather.6.cloned.1.call-start = ((), (), s32[]{:S(2)}) async-start(), calls=%async_computation.3 | async-start | bytes 1310720 | tf_op jit(solution)/shard_map/all_gather | solution.py:107
  68.1 94.3 %all-gather.4.cloned.1.call-start = ((), (), s32[]{:S(2)}) async-start(), calls=%async_computation.2 | async-start | bytes 1310720 | tf_op jit(solution)/shard_map/all_gather | solution.py:108
  70.0 123.8 %all-reduce.5.cloned.1.call-start = ((), (), s32[]{:S(2)}) async-start(), calls=%async_computation.4 | async-start | bytes 2097152 | tf_op jit(solution)/shard_map/psum | solution.py:105
Sparse Core Ops, SparseCore 0:
  66.5 86.6 reduce-scatter.1
Sparse Core Ops, SparseCore 1:
  69.0 14.9 all-gather.5
  85.5 16.7 all-gather.3
  157.4 36.4 all-reduce.4
where the time goes:
time: 209 us; the launch traced here: 208 us
  waiting for transfers between devices  107 us (51%)
  local copies, waits for them, and re-layouts  34.9 us (17%)
  loops' own time  18.3 us (9%)
  between operations  16.4 us (8%)
  other arithmetic  14 us (7%)
  blocking collectives  13.1 us (6%)
  matrix products  4.28 us (2%)
    reduce_scatter x1, waiting for transfers between devices, local(): lax.psum_scatter((product * grad_scale).astype(jnp.bfloat16), 'fsdp', sca...  75.5 us
    psum x1, waiting for transfers between devices, local(): summed = lax.psum(stepped, 'rep')  31.4 us
    unnamed x19, local copies, waits for them, and re-layouts  24 us
    another operation x1, loops' own time, entering(): return lax.fori_loop(0, peers, hop, start)  18.3 us
    all_gather x1, blocking collectives, entering(): everything = jax.tree.map(lambda part: lax.all_gather(part, axis), array)  13.1 us
    dynamic_slice x16, local copies, waits for them, and re-layouts, hop(): new = combine(before, jax.tree.map(lambda part: part[k], everything))  9.29 us
    dot_general x1, matrix products, local(): lax.dot_general(features, rotated, (((0,), (0,)), ((), ())), preferred_el...  4.28 us
  transfers between devices with their start and end apart: 4, of which 2 were waited for; matrix products, arithmetic and copies ran while one was open for 9% of the time, Pallas kernels for 0%

commit v1 on v0

--- a/solution.py
+++ b/solution.py
@@ -102,7 +102,7 @@
         grad, replica_params[0], first_moment[0], second_moment[0]
     )
     share_rows = anchor.shape[0]
-    summed = lax.psum(stepped, "rep")
+    summed = jnp.sum(lax.all_gather(stepped, "rep"), axis=0)
     anchor_rows, momentum_rows = (
         lax.all_gather(anchor, "rep", axis=0, tiled=True),
         lax.all_gather(momentum, "rep", axis=0, tiled=True),

time: 209 us -> 246 us (1.18)
  waiting for transfers between devices: 107 us -> 131 us
  local copies, waits for them, and re-layouts: 34.9 us -> 42 us
  other arithmetic: 14 us -> 18.2 us
  loops' own time: 18.3 us -> 21.3 us
    psum x1 -> x0, waiting for transfers between devices: 31.4 us -> none  [local(): summed = lax.psum(stepped, 'rep')]
    all_gather x0 -> x1, waiting for transfers between devices: none -> 26.4 us  [local(): summed = jnp.sum(lax.all_gather(stepped, 'rep'), axis=0)]
    all_gather x1, waiting for transfers between devices: 0.01 us -> 18.9 us  [local(): lax.all_gather(anchor, 'rep', axis=0, tiled=True)]
    all_gather x1, waiting for transfers between devices: 0.01 us -> 6.75 us  [local(): lax.all_gather(momentum, 'rep', axis=0, tiled=True)]
    all_gather x0 -> x1, local copies, waits for them, and re-layouts: none -> 6.02 us  [local(): summed = jnp.sum(lax.all_gather(stepped, 'rep'), axis=0)]
    reduce_sum x0 -> x1, other arithmetic: none -> 5.74 us  [local(): summed = jnp.sum(lax.all_gather(stepped, 'rep'), axis=0)]
    reduce_scatter x1, waiting for transfers between devices: 75.5 us -> 79.1 us  [local(): lax.psum_scatter((product * grad_scale).astype(jnp.bfloat16), 'fsdp', sca...]
    another operation x1, loops' own time: 18.3 us -> 21.3 us  [entering(): return lax.fori_loop(0, peers, hop, start)]
  transfers between devices with their start and end apart: 4 -> 4, of which waited for: 2 -> 4; matrix products, arithmetic and copies ran while one was open for 9% -> 11% of each run, Pallas kernels for 0% -> 0%
where the time goes in v1:
time: 246 us; the launch traced here: 245 us
  waiting for transfers between devices  131 us (53%)
  local copies, waits for them, and re-layouts  42 us (17%)
  loops' own time  21.3 us (9%)
  other arithmetic  18.2 us (7%)
  between operations  14.5 us (6%)
  blocking collectives  13.1 us (5%)
  matrix products  4.27 us (2%)
    reduce_scatter x1, waiting for transfers between devices, local(): lax.psum_scatter((product * grad_scale).astype(jnp.bfloat16), 'fsdp', sca...  79.1 us
    all_gather x1, waiting for transfers between devices, local(): summed = jnp.sum(lax.all_gather(stepped, 'rep'), axis=0)  26.4 us
    unnamed x19, local copies, waits for them, and re-layouts  23.4 us
    another operation x1, loops' own time, entering(): return lax.fori_loop(0, peers, hop, start)  21.3 us
    all_gather x1, waiting for transfers between devices, local(): lax.all_gather(anchor, 'rep', axis=0, tiled=True)  18.9 us
    all_gather x1, blocking collectives, entering(): everything = jax.tree.map(lambda part: lax.all_gather(part, axis), array)  13.1 us
    dynamic_slice x16, local copies, waits for them, and re-layouts, hop(): new = combine(before, jax.tree.map(lambda part: part[k], everything))  9.99 us
    all_gather x1, waiting for transfers between devices, local(): lax.all_gather(momentum, 'rep', axis=0, tiled=True)  6.75 us
  transfers between devices with their start and end apart: 4, of which 4 were waited for; matrix products, arithmetic and copies ran while one was open for 11% of the time, Pallas kernels for 0%

profile of v1, /device:TPU:0, one launch (start us, length us, event | category | flops | bytes accessed | tf_op | source)
XLA Modules:
  0.0 244.9 jit_solution(18047215226848955010)
XLA Ops:
  7.2 0.0 copy-start
  7.2 0.0 reduce-scatter.2.cloned.1.call-start
  7.2 1.5 slice.28
  8.7 0.8 compare_reduce_fusion
  9.6 1.4 compare_reduce_fusion.2
  11.0 0.6 select_reduce_fusion
  12.2 1.2 dynamic-slice
  13.5 1.4 bitcast_dynamic-update-slice_fusion
  14.9 0.8 dynamic-update-slice.1
  15.6 13.1 %all-reduce.2 = (s32[8]{0:T(128)S(1)}, s32[8]{0:T(128)S(1)}) all-reduce(s32[8]{0:T(128)S(1)} %bitcast_dynamic-update-slice_fusion, s32[8]{0:T(128)S(1)} %dynamic-update-slice.1), channel_id=2, replica_groups=mesh['rep'=4,'fsdp'=8] {'fsdp'}, use_global_device_ids=true, to_apply=%add | all-reduce | flops 16 | bytes 128 | tf_op jit(solution)/shard_map/all_gather | solution.py:14
  28.7 31.3 %while.15 = (s32[]{:T(128)}, s32[]{:T(128)}, s32[]{:T(128)}, s32[]{:T(128)}, s32[8]{0:T(128)S(1)}, /*index=5*/s32[8]{0:T(128)S(1)}, s32[]{:T(128)}, s32[]{:T(128)}) while((s32[]{:T(128)}, s32[]{:T(128)}, s32[]{:T(128)}, s32[]{:T(128)}, s32[8]{0:T(128)S(1)}, /*index=5*/s32[8]{0:T(128)S(1)}, s32[]{:T(128)}, s32[]{:T(128)}) %tuple.40), condition=%wide.region_2.3_spmd, body=%wide.region_1.2_spmd.sunk | while | flops 10 | bytes 201 | solution.py:26
  28.7 0.7 dynamic_slice.21
  30.0 0.6 dynamic_slice.22
  32.6 0.7 dynamic_slice.21
  34.0 0.6 dynamic_slice.22
  36.5 0.7 dynamic_slice.21
  37.9 0.6 dynamic_slice.22
  40.4 0.7 dynamic_slice.21
  41.8 0.6 dynamic_slice.22
  44.3 0.7 dynamic_slice.21
  45.7 0.6 dynamic_slice.22
  48.2 0.7 dynamic_slice.21
  49.6 0.6 dynamic_slice.22
  52.2 0.7 dynamic_slice.21
  53.5 0.6 dynamic_slice.22
  56.1 0.7 dynamic_slice.21
  57.4 0.6 dynamic_slice.22
  60.0 0.7 compare_reduce_fusion.1
  60.7 0.1 add_select_fusion
  60.8 0.3 reduce-window.9
  61.1 0.1 slice.32
  61.2 0.1 slice_reduce_fusion
  61.3 1.2 copy.24
  62.5 0.1 convert.9
  62.6 0.1 fusion.9
  62.7 0.4 multiply_cosine_fusion
  63.1 0.1 add_convert_fusion
  63.3 0.0 copy-done
  63.3 4.3 %fusion = bf16[4096,512]{0,1:T(8,128)(2,1)} fusion(bf16[384,512]{0,1:T(8,128)(2,1)S(1)} %bitcast.58, bf16[1,384,4096]{2,1,0:T(8,128)(2,1)S(1)} %copy-done), kind=kOutput, calls=%fused_computation.1 | convolution fusion | flops 1614807040 | bytes 7733248 | tf_op jit(solution)/shard_map/dot_general | solution.py:95
  67.5 0.0 reduce-scatter.2.cloned.1.call-update
  67.6 0.0 all-gather.10.cloned.1.call-start
  67.6 2.5 %copy.23 = f32[1,512,512]{1,2,0:T(8,128)} copy(f32[1,512,512]{2,1,0:T(8,128)} %param.14) | data formatting | bytes 2097152 | tf_op args[4]
  70.1 2.5 %copy.25 = f32[1,512,512]{1,2,0:T(8,128)} copy(f32[1,512,512]{2,1,0:T(8,128)} %param.15) | data formatting | bytes 2097152 | tf_op args[5]
  72.7 2.6 %copy.28 = f32[1,512,512]{1,2,0:T(8,128)} copy(f32[1,512,512]{2,1,0:T(8,128)} %param.13) | data formatting | bytes 2097152 | tf_op args[3]
  75.3 79.1 %reduce-scatter.2.cloned.1.call-done = bf16[512,512]{0,1:T(8,128)(2,1)} async-done(((bf16[4096,512]{0,1:T(8,128)(2,1)}), bf16[512,512]{0,1:T(8,128)(2,1)}) %reduce-scatter.2.cloned.1.call-update) | async-done | bytes 524304 | tf_op jit(solution)/shard_map/reduce_scatter | solution.py:98
  154.4 4.1 %bitcast_subtract_fusion = (f32[512,512]{0,1:T(8,128)}, f32[1,512,512]{1,2,0:T(8,128)}, f32[1,512,512]{1,2,0:T(8,128)}) fusion(f32[1,512,512]{1,2,0:T(8,128)} %copy.28, bf16[512,512]{0,1:T(8,128)(2,1)} %reduce-scatter.2.cloned.1.call-done, f32[1,512,512]{1,2,0:T(8,128)} %copy.23, f32[1,512,512]{1,2,0:T(8,128)} %copy.25), kind=kLoop, calls=%fused_computation.7 | loop fusion | flops 3670016 | bytes 6815744 | tf_op jit(solution)/shard_map/sub | solution.py:53
  158.6 0.0 all-gather.10.cloned.1.call-update
  158.6 0.0 all-gather.6.cloned.1.call-start
  158.6 0.9 copy.26
  159.5 0.0 all-gather.6.cloned.1.call-update
  159.5 0.0 all-gather.8.cloned.1.call-start
  159.6 1.8 copy.27
  161.4 0.0 all-gather.8.cloned.1.call-update
  161.4 2.5 %copy.29 = f32[1,512,512]{2,1,0:T(8,128)} copy(f32[1,512,512]{1,2,0:T(8,128)} %get-tuple-element.146) | data formatting | bytes 2097152
  163.9 2.6 %copy.30 = f32[1,512,512]{2,1,0:T(8,128)} copy(f32[1,512,512]{1,2,0:T(8,128)} %get-tuple-element.145) | data formatting | bytes 2097152
  166.5 26.4 %all-gather.10.cloned.1.call-done = f32[2048,512]{0,1:T(8,128)} async-done(((f32[512,512]{0,1:T(8,128)}), f32[2048,512]{0,1:T(8,128)}) %all-gather.10.cloned.1.call-update) | async-done | bytes 4194320 | tf_op jit(solution)/shard_map/all_gather | solution.py:105
  193.0 6.0 %reshape.127 = f32[4,512,512]{1,0,2:T(4,128)} reshape(f32[2048,512]{0,1:T(8,128)} %all-gather.10.cloned.1.call-done) | data formatting | bytes 8388608 | tf_op jit(solution)/shard_map/all_gather | solution.py:105
  199.0 5.7 %reduce_sum.9 = f32[512,512]{0,1:T(8,128)} reduce(f32[4,512,512]{1,0,2:T(4,128)} %reshape.127, f32[]{:T(128)} %constant.66.clone.1), dimensions={0}, to_apply=%region_6.7 | reduce | flops 786432 | bytes 5242884 | tf_op jit(solution)/shard_map/reduce_sum | solution.py:105
  204.7 6.8 %all-gather.6.cloned.1.call-done = f32[512,512]{0,1:T(8,128)} async-done(((f32[128,512]{0,1:T(8,128)}), f32[512,512]{0,1:T(8,128)}) %all-gather.6.cloned.1.call-update) | async-done | bytes 1048592 | tf_op jit(solution)/shard_map/all_gather | solution.py:108
  211.5 18.9 %all-gather.8.cloned.1.call-done = f32[512,512]{0,1:T(8,128)} async-done(((f32[128,512]{0,1:T(8,128)}), f32[512,512]{0,1:T(8,128)}) %all-gather.8.cloned.1.call-update) | async-done | bytes 1048592 | tf_op jit(solution)/shard_map/all_gather | solution.py:107
  230.4 3.6 %multiply_subtract_fusion = (f32[512,512]{0,1:T(8,128)}, f32[512,512]{0,1:T(8,128)}) fusion(f32[512,512]{0,1:T(8,128)} %all-gather.8.cloned.1.call-done, f32[512,512]{0,1:T(8,128)} %reduce_sum.9, f32[512,512]{0,1:T(8,128)} %all-gather.6.cloned.1.call-done), kind=kLoop, calls=%fused_computation.11 | loop fusion | flops 2097152 | bytes 5242880 | tf_op jit(solution)/shard_map/sub | solution.py:112
  234.1 2.5 %copy.32 = f32[512,512]{1,0:T(8,128)} copy(f32[512,512]{0,1:T(8,128)} %get-tuple-element.142) | data formatting | bytes 2097152
  236.6 1.0 constant_dynamic-slice_fusion
  237.6 0.8 copy.31
  (7 shorter events, 0.1 us)
Async XLA Ops:
  7.2 56.1 %copy-start = (bf16[1,384,4096]{2,1,0:T(8,128)(2,1)S(1)}, bf16[1,384,4096]{2,1,0:T(8,128)(2,1)}, u32[]{:S(2)}) copy-start(bf16[1,384,4096]{2,1,0:T(8,128)(2,1)} %param.10) | copy-start | bytes 9437188
  7.2 147.2 %reduce-scatter.2.cloned.1.call-start = ((), (), s32[]{:S(2)}) async-start(), calls=%async_computation.1 | async-start | bytes 4718592 | tf_op jit(solution)/shard_map/reduce_scatter | solution.py:98
  67.6 125.4 %all-gather.10.cloned.1.call-start = ((), (), s32[]{:S(2)}) async-start(), calls=%async_computation.4 | async-start | bytes 5242880 | tf_op jit(solution)/shard_map/all_gather | solution.py:105
  75.3 83.4 %copy-start.1 = (f32[128,512]{1,0:T(8,128)S(1)}, f32[128,512]{1,0:T(8,128)}, u32[]{:S(2)}) copy-start(f32[128,512]{1,0:T(8,128)} %param.17) | copy-start | bytes 786436
  158.6 52.9 %all-gather.6.cloned.1.call-start = ((), (), s32[]{:S(2)}) async-start(), calls=%async_computation.2 | async-start | bytes 1310720 | tf_op jit(solution)/shard_map/all_gather | solution.py:108
  159.5 70.9 %all-gather.8.cloned.1.call-start = ((), (), s32[]{:S(2)}) async-start(), calls=%async_computation.3 | async-start | bytes 1310720 | tf_op jit(solution)/shard_map/all_gather | solution.py:107
Sparse Core Ops, SparseCore 0:
  67.7 86.6 reduce-scatter.1
  158.7 34.2 all-gather.9
  194.6 16.8 all-gather.5
  213.5 16.8 all-gather.7
